TPU v7x, 32 devices: a whole 2x2x4 slice. The times are simulated.
32 devices in a mesh: wave: 8 (over y, x, core), lev: 4 (over z).
Axes of the slice: x: 2, y: 2, z: 4, core: 2. Of those that a mesh axis runs over, the one named last changes fastest.
Arguments:
- coefficients: bfloat16 [640, 640, 512], P('wave', 'lev'), may hold values from -6 to 6
- factors: bfloat16 [3, 2, 640, 80, 640], P(None, None, 'wave', None, 'lev'), may hold values from -0.5 to 0.5
- wave_ids: int32 [640], replicated, may hold values from 0 to 639, each once
Outputs:
- grid: bfloat16 [640, 256, 2560], P(('wave', 'lev'))
Inputs may be any that keep to these rules, and one draw needn't show every extreme that they name: `wave_ids`: each wavenumber 0 .. 639 appears exactly once.
All inputs are finite; a program needn't handle non-finite values.
Results may differ from a plain program's by a relative error of at most 0.0079.
Values may be sent and summed in bfloat16 or wider, within the bound.
A program may use at most 192 MiB of HBM per device.

v0:
```python
import functools
import math

import jax
import jax.numpy as jnp
from jax import lax
from jax.experimental import pallas as pl
from jax.experimental.pallas import tpu as pltpu
from jax.sharding import PartitionSpec as P


NLON = 2560
UNIT = 16


def swapped(block, axis, apart):
    count = lax.axis_size(axis)
    route = []
    for low in range(count):
        high = low | 1 << apart
        if high != low and high < count:
            route += [(low, high), (high, low)]
    return lax.ppermute(block, axis, route)


def combine_kernel(count, factor_ref, own_ref, partner_ref, *refs):
    out_ref = refs[-1]
    for m in range(count):
        total = jnp.dot(factor_ref[0, m], own_ref[m], preferred_element_type=jnp.float32)
        total += jnp.dot(factor_ref[1, m], partner_ref[m], preferred_element_type=jnp.float32)
        out_ref[m] = total.astype(out_ref.dtype)


def combine(factor, own, partner, start, after):
    slots, rows, channels = own.shape
    step = math.gcd(slots, 8)
    block = pl.BlockSpec((step, rows, channels), lambda i: (i, 0, 0))
    return pl.pallas_call(
        functools.partial(combine_kernel, step),
        grid=(slots // step,),
        out_shape=jax.ShapeDtypeStruct(own.shape, own.dtype),
        in_specs=[
            pl.BlockSpec((2, step, rows, rows), lambda i: (0, start // step + i, 0, 0)),
            block,
            block,
        ]
        + [pl.BlockSpec(memory_space=pl.ANY)] * len(after),
        out_specs=block,
        cost_estimate=pl.CostEstimate(
            flops=4 * slots * rows * rows * channels,
            bytes_accessed=2 * (3 * own.size + 2 * slots * rows * rows),
            transcendentals=0,
        ),
    )(factor, own, partner, *after)


def synthesis_kernel(count, *refs):
    table_ref, out_ref = refs[count], refs[count + 1]
    half = out_ref.shape[1]
    wide = jnp.concatenate([ref[0] for ref in refs[:count]], axis=0)
    turned = wide.T
    spectrum = jnp.concatenate([turned[:half], turned[half:]], axis=1)
    span = math.gcd(out_ref.shape[2], 512)
    for j in range(0, out_ref.shape[2], span):
        out_ref[0, :, j : j + span] = jnp.dot(
            spectrum, table_ref[:, j : j + span], preferred_element_type=jnp.float32
        ).astype(out_ref.dtype)


def synthesis(parts, table):
    rows, _, channels = parts[0].shape
    depth, longitudes = table.shape
    return pl.pallas_call(
        functools.partial(synthesis_kernel, len(parts)),
        grid=(rows,),
        out_shape=jax.ShapeDtypeStruct((rows, channels // 2, longitudes), parts[0].dtype),
        in_specs=[pl.BlockSpec((1, p.shape[1], channels), lambda i: (i, 0, 0)) for p in parts]
        + [pl.BlockSpec((depth, longitudes), lambda i: (0, 0), pipeline_mode=pl.Buffered(1))],
        out_specs=pl.BlockSpec((1, channels // 2, longitudes), lambda i: (i, 0, 0)),
        cost_estimate=pl.CostEstimate(
            flops=rows * channels * depth * longitudes,
            bytes_accessed=rows * channels * (depth + longitudes) + 2 * table.size,
            transcendentals=0,
        ),
    )(*parts, table)


def cuts_of(slots):
    unit = math.gcd(slots, 16)
    edges = [0]
    while edges[-1] < slots:
        left = slots - edges[-1]
        edges.append(edges[-1] + (unit if edges[-1] == 0 or left <= 2 * unit else 2 * unit))
    return list(zip(edges[:-1], edges[1:]))


def mixes(pieces, sections):
    return [
        (t - s - (s > 0), s)
        for t in range(pieces + sections + 1)
        for s in range(sections)
        if 0 <= t - s - (s > 0) < pieces
    ]


def body(coefficients, factors, wave_ids):
    wave_count = lax.axis_size("wave")
    lev_count = lax.axis_size("lev")
    sections = wave_count.bit_length() - 1
    rows, slots, _ = coefficients.shape
    total_waves = wave_ids.shape[0]
    wave_pos = lax.axis_index("wave")
    lev_pos = lax.axis_index("lev")
    cuts = cuts_of(slots)
    pieces = len(cuts)
    band = rows // lev_count
    ids = [
        lax.dynamic_slice_in_dim(wave_ids, (lev_pos - d) % lev_count * slots, slots, 0)
        for d in range(lev_count)
    ]
    degree = wave_pos * rows + jnp.arange(rows, dtype=jnp.int32)
    factor = [factors[s].transpose(0, 3, 1, 2) for s in range(sections)]

    current = [None] * pieces
    gathered = [None] * pieces

    def start(c):
        low, high = cuts[c]
        live = (degree[:, None] >= ids[0][low:high][None, :])[:, :, None]
        block = coefficients[:, low:high, :]
        block = jnp.where(live, block, jnp.zeros((), block.dtype))
        return block.transpose(1, 0, 2)

    def spread(c):
        ready = current[c].transpose(1, 0, 2)
        got = [lax.dynamic_slice_in_dim(ready, lev_pos * band, band, 0)]
        for d in range(1, lev_count):
            part = lax.dynamic_slice_in_dim(ready, (lev_pos + d) % lev_count * band, band, 0)
            route = [(k, (k + d) % lev_count) for k in range(lev_count)]
            got.append(lax.ppermute(part, "lev", route))
        gathered[c] = got

    for c in range(pieces):
        current[c] = start(c)
    after = []
    for c, s in mixes(pieces, sections):
        partner = swapped(current[c], "wave", s)
        current[c] = combine(factor[s], current[c], partner, cuts[c][0], after)
        after = [current[c]]
        if s == sections - 1:
            spread(c)

    table_ids = jnp.concatenate([ids[d][low:high] for low, high in cuts for d in range(lev_count)])
    longitude = jnp.arange(NLON, dtype=jnp.int32)
    phases = table_ids[:, None] * longitude[None, :] % NLON
    angles = phases.astype(jnp.float32) * (2.0 * math.pi / NLON)
    weight = jnp.where(table_ids == 0, 1.0, 2.0).astype(jnp.float32) / math.sqrt(2.0 * total_waves)
    cosine_part = (weight[:, None] * jnp.cos(angles)).astype(jnp.bfloat16)
    sine_part = (-weight[:, None] * jnp.sin(angles)).astype(jnp.bfloat16)
    table = jnp.concatenate([cosine_part, sine_part], axis=0)

    return synthesis([part for got in gathered for part in got], table)


def whole(coefficients, factors, wave_ids):
    return body(coefficients, factors, wave_ids)


MESH = pl.DeviceIdType.MESH
RING = 3


def exchange_kernel(
    unit,
    ids_ref,
    coef_ref,
    factor_ref,
    bands_ref,
    coef_in,
    factor_in,
    factor_f32,
    factor,
    turn,
    mixed,
    ready,
    coef_sem,
    factor_sem,
    send_sem,
    recv_sem,
    band_send,
    band_recv,
    band_own,
    free_sem,
):
    wave_pos, lev_pos = lax.axis_index("wave"), lax.axis_index("lev")
    lev_count = lax.axis_size("lev")
    rows, slots, channels = coef_ref.shape
    sections = factor_ref.shape[0]
    chunks = slots // unit
    band = rows // lev_count
    group = factor_in.shape[2]
    groups = rows // group
    jobs = sections * groups
    lane = 128

    def other(s):
        bit = 1 << s
        return jnp.where(wave_pos // bit % 2 == 0, wave_pos + bit, wave_pos - bit)

    def peer(d):
        return lax.rem(lev_pos + d, lev_count)

    barrier = pltpu.get_barrier_semaphore()
    for s in range(sections):
        pl.semaphore_signal(barrier, inc=1, device_id={"wave": other(s)}, device_id_type=MESH)
    for d in range(1, lev_count):
        pl.semaphore_signal(barrier, inc=1, device_id={"lev": peer(d)}, device_id_type=MESH)

    def coef_copy(c):
        k = lax.rem(c, 2)
        return pltpu.make_async_copy(
            coef_ref.at[:, pl.ds(pl.multiple_of(c * unit, unit), unit), :], coef_in.at[k], coef_sem.at[k]
        )

    def factor_copy(j):
        k = lax.rem(j, 2)
        s, g = lax.div(j, groups), lax.rem(j, groups)
        return pltpu.make_async_copy(
            factor_ref.at[s, :, pl.ds(g * group, group)], factor_in.at[k], factor_sem.at[k]
        )

    for k in range(2):
        coef_copy(k).start()
        factor_copy(k).start()

    def slot(s, c):
        return s * RING + lax.rem(c, RING)

    def swap(s, c):
        k = slot(s, c)
        return pltpu.make_async_remote_copy(
            src_ref=mixed.at[k, :, pl.ds(0, rows), :],
            dst_ref=mixed.at[k, :, pl.ds(rows, rows), :],
            send_sem=send_sem.at[k],
            recv_sem=recv_sem.at[k],
            device_id={"wave": other(s)},
            device_id_type=MESH,
        )

    def band_copy(d, c, owner):
        k = lax.rem(c, RING)
        return pltpu.make_async_remote_copy(
            src_ref=ready.at[k, pl.ds(peer(d) * band, band)],
            dst_ref=bands_ref.at[:, pl.ds(pl.multiple_of(owner * slots + c * unit, unit), unit), :],
            send_sem=band_send.at[k, d - 1],
            recv_sem=band_recv.at[c, d - 1],
            device_id={"lev": peer(d)},
            device_id_type=MESH,
        )

    def own_copy(c):
        k = lax.rem(c, RING)
        return pltpu.make_async_copy(
            ready.at[k, pl.ds(lev_pos * band, band)],
            bands_ref.at[:, pl.ds(pl.multiple_of(lev_pos * slots + c * unit, unit), unit), :],
            band_own.at[k],
        )

    def release(s, c):
        @pl.when(c >= RING)
        def _():
            swap(s, c - RING).wait_send()

    def send(s, c):
        @pl.when(c >= RING)
        def _():
            pl.semaphore_wait(free_sem.at[s], 1)

        swap(s, c).start()

    degree = wave_pos * rows + lax.broadcasted_iota(jnp.int32, (rows, lane), 0)

    def begin(c):
        coef_copy(c).wait()
        for n, low in enumerate(range(0, channels, lane)):
            part = coef_in[lax.rem(c, 2), :, :, pl.ds(low, lane)].astype(jnp.float32)
            turn[n] = part.reshape(rows * unit, lane)

        @pl.when(c + 2 < chunks)
        def _():
            coef_copy(c + 2).start()

        release(0, c)
        k = slot(0, c)
        for m in range(unit):
            live = degree >= ids_ref[pl.ds(c * unit + m, 1), :]
            for n, low in enumerate(range(0, channels, lane)):
                part = turn[n, pl.ds(m, rows, stride=unit), :]
                part = jnp.where(live, part, 0.0)
                mixed[k, m, pl.ds(0, rows), pl.ds(low, lane)] = part.astype(mixed.dtype)
        send(0, c)

    def prepare(s):
        def job(g, carry):
            j = s * groups + g
            factor_copy(j).wait()
            k = lax.rem(j, 2)
            for o in range(group):
                both = jnp.concatenate([factor_in[k, 0, o], factor_in[k, 1, o]], axis=0)
                rest = jnp.zeros((2 * lane - 2 * rows, slots), both.dtype)
                for n, part in enumerate((both[:lane], jnp.concatenate([both[lane:], rest], axis=0))):
                    factor_f32[n, pl.ds(o, slots, stride=group), :] = part.T.astype(jnp.float32)

            @pl.when(j + 2 < jobs)
            def _():
                factor_copy(j + 2).start()

            low = pl.multiple_of(g * group, group)
            for n in range(2):
                factor[pl.ds(s * slots, slots), pl.ds(low, group), pl.ds(n * lane, lane)] = (
                    factor_f32[n].astype(factor.dtype).reshape(slots, group, lane)
                )
            return carry

        lax.fori_loop(0, groups, job, 0)

    def mix(s, c):
        k = slot(s, c)
        swap(s, c).wait_recv()
        last = s == sections - 1
        if last:

            @pl.when(c >= RING)
            def _():
                for d in range(1, lev_count):
                    band_copy(d, c - RING, lev_pos).wait_send()
                own_copy(c - RING).wait()

        else:
            release(s + 1, c)
        for m in range(unit):
            total = jnp.dot(
                factor[s * slots + c * unit + m][:, : 2 * rows], mixed[k, m], preferred_element_type=jnp.float32
            )
            if last:
                for n, low in enumerate(range(0, channels, lane)):
                    turn[n, pl.ds(m, rows, stride=unit), :] = total[:, low : low + lane]
            else:
                mixed[slot(s + 1, c), m, pl.ds(0, rows), :] = total.astype(mixed.dtype)

        @pl.when(c < chunks - RING)
        def _():
            pl.semaphore_signal(free_sem.at[s], inc=1, device_id={"wave": other(s)}, device_id_type=MESH)

        if last:
            for n, low in enumerate(range(0, channels, lane)):
                ready[lax.rem(c, RING), :, :, pl.ds(low, lane)] = (
                    turn[n].astype(ready.dtype).reshape(rows, unit, lane)
                )
            for d in (lev_count // 2, 1, lev_count - 1) if lev_count == 4 else range(1, lev_count):
                band_copy(d, c, lev_pos).start()
            own_copy(c).start()
        else:
            send(s + 1, c)

    def guarded(s, c):
        @pl.when((c >= 0) & (c < chunks))
        def _():
            mix(s, c)

    pl.semaphore_wait(barrier, sections + lev_count - 1)

    def step(t, carry):
        guarded(0, t - 1)

        @pl.when(t < chunks)
        def _():
            begin(t)

        for s in range(1, sections - 1):
            guarded(s, t - 1 - s)

        @pl.when(t < sections)
        def _():
            prepare(t)

        guarded(sections - 1, t - sections)
        return carry

    lax.fori_loop(0, chunks + sections, step, 0)

    for c in range(chunks - RING, chunks):
        for s in range(sections):
            swap(s, jnp.int32(c)).wait_send()
        for d in range(1, lev_count):
            band_copy(d, jnp.int32(c), lev_pos).wait_send()
        own_copy(jnp.int32(c)).wait()

    def arrived(c, carry):
        for d in range(1, lev_count):
            band_copy(d, c, peer(lev_count - d)).wait_recv()
        return carry

    lax.fori_loop(0, chunks, arrived, 0)


def exchange(ids, coefficients, factors, unit):
    lev_count = lax.axis_size("lev")
    rows, slots, channels = coefficients.shape
    sections = factors.shape[0]
    chunks = slots // unit
    kind = coefficients.dtype
    group = 16
    return pl.pallas_call(
        functools.partial(exchange_kernel, unit),
        out_shape=jax.ShapeDtypeStruct((rows // lev_count, lev_count * slots, channels), kind),
        in_specs=[
            pl.BlockSpec(memory_space=pltpu.VMEM),
            pl.BlockSpec(memory_space=pltpu.HBM),
            pl.BlockSpec(memory_space=pltpu.HBM),
        ],
        out_specs=pl.BlockSpec(memory_space=pltpu.HBM),
        scratch_shapes=[
            pltpu.VMEM((2, rows, unit, channels), kind),
            pltpu.VMEM((2, 2, group, rows, slots), kind),
            pltpu.VMEM((2, slots * group, 128), jnp.float32),
            pltpu.VMEM((sections * slots, rows, 256), kind),
            pltpu.VMEM((channels // 128, rows * unit, 128), jnp.float32),
            pltpu.VMEM((sections * RING, unit, 2 * rows, channels), kind),
            pltpu.VMEM((RING, rows, unit, channels), kind),
            pltpu.SemaphoreType.DMA((2,)),
            pltpu.SemaphoreType.DMA((2,)),
            pltpu.SemaphoreType.DMA((sections * RING,)),
            pltpu.SemaphoreType.DMA((sections * RING,)),
            pltpu.SemaphoreType.DMA((RING, lev_count - 1)),
            pltpu.SemaphoreType.DMA((chunks, lev_count - 1)),
            pltpu.SemaphoreType.DMA((RING,)),
            pltpu.SemaphoreType.REGULAR((sections,)),
        ],
        compiler_params=pltpu.CompilerParams(
            collective_id=0, has_side_effects=True, vmem_limit_bytes=60 << 20
        ),
    )(ids, coefficients, factors)


def grid_kernel(cos_a, sin_a, cos_b, sin_b, u_ref, out_ref, table):
    slots = cos_a.shape[0]
    half = out_ref.shape[1]
    lane = cos_b.shape[1]

    @pl.when(pl.program_id(0) == 0)
    def _():
        for j in range(out_ref.shape[2] // lane):
            ca, sa = cos_a[:, j : j + 1], sin_a[:, j : j + 1]
            table[:slots, j * lane : (j + 1) * lane] = (ca * cos_b[...] - sa * sin_b[...]).astype(table.dtype)
            table[slots:, j * lane : (j + 1) * lane] = (-(sa * cos_b[...] + ca * sin_b[...])).astype(table.dtype)

    turned = u_ref[0].T
    spectrum = jnp.concatenate([turned[:half], turned[half:]], axis=1)
    span = math.gcd(out_ref.shape[2], 512)
    for j in range(0, out_ref.shape[2], span):
        out_ref[0, :, j : j + span] = jnp.dot(
            spectrum, table[:, j : j + span], preferred_element_type=jnp.float32
        ).astype(out_ref.dtype)


def grid_of(wave_ids, bands):
    rows, slots, channels = bands.shape
    lane = 128

    def angle(j):
        phases = wave_ids[:, None] * j[None, :] % NLON
        return phases.astype(jnp.float32) * (2.0 * math.pi / NLON)

    weight = jnp.where(wave_ids == 0, 1.0, 2.0).astype(jnp.float32) / math.sqrt(2.0 * wave_ids.shape[0])
    a = angle(lane * jnp.arange(NLON // lane, dtype=jnp.int32))
    b = angle(jnp.arange(lane, dtype=jnp.int32))
    parts = [weight[:, None] * jnp.cos(a), weight[:, None] * jnp.sin(a), jnp.cos(b), jnp.sin(b)]
    return pl.pallas_call(
        grid_kernel,
        grid=(rows,),
        out_shape=jax.ShapeDtypeStruct((rows, channels // 2, NLON), bands.dtype),
        in_specs=[pl.BlockSpec(p.shape, lambda i: (0, 0), pipeline_mode=pl.Buffered(1)) for p in parts]
        + [pl.BlockSpec((1, slots, channels), lambda i: (i, 0, 0))],
        out_specs=pl.BlockSpec((1, channels // 2, NLON), lambda i: (i, 0, 0)),
        scratch_shapes=[pltpu.VMEM((2 * slots, NLON), bands.dtype)],
        cost_estimate=pl.CostEstimate(
            flops=2 * rows * channels * slots * NLON,
            bytes_accessed=2 * bands.size + rows * channels * NLON,
            transcendentals=0,
        ),
    )(*parts, bands)


def unit_of(rows, slots):
    return UNIT if rows % 16 == 0 and 128 <= 2 * rows <= 256 and slots % UNIT == 0 and slots // UNIT > RING else 0


def staged(coefficients, factors, wave_ids):
    rows, slots, _ = coefficients.shape
    ids = lax.dynamic_slice_in_dim(wave_ids, lax.axis_index("lev") * slots, slots, 0)
    ids = jnp.broadcast_to(ids[:, None], (slots, 128))
    bands = exchange(ids, coefficients, factors, unit_of(rows, slots))
    return grid_of(wave_ids, bands)


def solution(mesh):
    in_specs = (P("wave", "lev", None), P(None, None, "wave", None, "lev"), P())
    out_specs = P(("wave", "lev"), None, None)

    def mapped(step):
        return jax.shard_map(step, mesh=mesh, in_specs=in_specs, out_specs=out_specs, check_vma=False)

    def run(coefficients, factors, wave_ids):
        lev_count = mesh.shape["lev"]
        slots = coefficients.shape[1] // lev_count
        if unit_of(factors.shape[3], slots):
            return mapped(staged)(coefficients, factors, wave_ids)
        return mapped(whole)(coefficients, factors, wave_ids)

    return run
```

profile of v0, /device:TPU:9, one launch (start us, length us, event | category | flops | bytes accessed | tf_op | source)
XLA Modules:
  0.0 407.4 jit_solution(1596652416072673343)
XLA Ops:
  0.0 0.8 dynamic_slice.3
  0.8 0.7 select_multiply_fusion
  1.5 0.7 broadcast_in_dim.12.ids_ref
  2.2 3.0 sine_multiply_fusion
  5.2 2.9 fusion.6
  8.1 355.0 %shard_map.37.u_ref = bf16[20,640,512]{2,1,0:T(8,128)(2,1)} custom-call(s32[160,128]{1,0:T(8,128)} %broadcast_in_dim.12.ids_ref, bf16[80,160,512]{2,1,0:T(8,128)(2,1)} %coef_ref.1, bf16[3,2,80,80,160]{4,3,2,1,0:T(8,128)(2,1)} %factor_ref.1), custom_call_target="tpu_custom_call" | custom-call | tf_op jit(solution)/shard_map/pallas_call | solution.py:414
  363.1 44.3 %shard_map.38 = bf16[20,256,2560]{2,1,0:T(8,128)(2,1)} custom-call(f32[640,20]{1,0:T(8,128)} %get-tuple-element.6.cos_a, f32[640,20]{1,0:T(8,128)} %get-tuple-element.5.sin_a, f32[640,128]{1,0:T(8,128)} %get-tuple-element.8.cos_b, f32[640,128]{1,0:T(8,128)} %get-tuple-element.7.sin_b, bf16[20,640,512]{2,1,0:T(8,128)(2,1)} %shard_map.37.u_ref), custom_call_target="tpu_custom_call" | custom-call | flops 33554432000 | bytes 39321600 | tf_op jit(solution)/shard_map/pallas_call | solution.py:479
  (1 shorter events, 0.0 us)
where the time goes:
time: 409 us; the launch traced here: 407 us
  Pallas kernels  399 us (98%)
  other arithmetic  6.6 us (2%)
    pallas_call x1, Pallas kernels, exchange(): pl.pallas_call(functools.partial(exchange_kernel, unit), out_shape=jax.Sh...  355 us
    pallas_call x1, Pallas kernels, grid_of(): pl.pallas_call(grid_kernel, grid=(rows,), out_shape=jax.ShapeDtypeStruct(...  44.3 us

commit v1 on v0

--- a/solution.py
+++ b/solution.py
@@ -10,7 +10,9 @@
 
 
 NLON = 2560
-UNIT = 16
+UNIT = 8
+SPLIT = 2
+EARLY = 12
 
 
 def swapped(block, axis, apart):
@@ -172,10 +174,13 @@
 
 def exchange_kernel(
     unit,
+    early,
     ids_ref,
     coef_ref,
     factor_ref,
     bands_ref,
+    partial_ref,
+    later_ref,
     coef_in,
     factor_in,
     factor_f32,
@@ -183,6 +188,9 @@
     turn,
     mixed,
     ready,
+    table,
+    row_in,
+    row_out,
     coef_sem,
     factor_sem,
     send_sem,
@@ -190,14 +198,20 @@
     band_send,
     band_recv,
     band_own,
+    row_sem,
+    out_sem,
+    table_sem,
     free_sem,
 ):
     wave_pos, lev_pos = lax.axis_index("wave"), lax.axis_index("lev")
     lev_count = lax.axis_size("lev")
     rows, slots, channels = coef_ref.shape
     sections = factor_ref.shape[0]
-    chunks = slots // unit
+    width = coef_in.shape[3]
+    split = channels // width
+    chunks = slots // unit * split
     band = rows // lev_count
+    longitudes = table.shape[1]
     group = factor_in.shape[2]
     groups = rows // group
     jobs = sections * groups
@@ -216,11 +230,13 @@
     for d in range(1, lev_count):
         pl.semaphore_signal(barrier, inc=1, device_id={"lev": peer(d)}, device_id_type=MESH)
 
+    def place(c):
+        low = pl.multiple_of(lax.div(c, split) * unit, unit)
+        return pl.ds(low, unit), pl.ds(pl.multiple_of(lax.rem(c, split) * width, width), width)
+
     def coef_copy(c):
         k = lax.rem(c, 2)
-        return pltpu.make_async_copy(
-            coef_ref.at[:, pl.ds(pl.multiple_of(c * unit, unit), unit), :], coef_in.at[k], coef_sem.at[k]
-        )
+        return pltpu.make_async_copy(coef_ref.at[(slice(None), *place(c))], coef_in.at[k], coef_sem.at[k])
 
     def factor_copy(j):
         k = lax.rem(j, 2)
@@ -251,7 +267,7 @@
         k = lax.rem(c, RING)
         return pltpu.make_async_remote_copy(
             src_ref=ready.at[k, pl.ds(peer(d) * band, band)],
-            dst_ref=bands_ref.at[:, pl.ds(pl.multiple_of(owner * slots + c * unit, unit), unit), :],
+            dst_ref=bands_ref.at[(slice(None), owner, *place(c))],
             send_sem=band_send.at[k, d - 1],
             recv_sem=band_recv.at[c, d - 1],
             device_id={"lev": peer(d)},
@@ -262,7 +278,7 @@
         k = lax.rem(c, RING)
         return pltpu.make_async_copy(
             ready.at[k, pl.ds(lev_pos * band, band)],
-            bands_ref.at[:, pl.ds(pl.multiple_of(lev_pos * slots + c * unit, unit), unit), :],
+            bands_ref.at[(slice(None), lev_pos, *place(c))],
             band_own.at[k],
         )
 
@@ -282,7 +298,7 @@
 
     def begin(c):
         coef_copy(c).wait()
-        for n, low in enumerate(range(0, channels, lane)):
+        for n, low in enumerate(range(0, width, lane)):
             part = coef_in[lax.rem(c, 2), :, :, pl.ds(low, lane)].astype(jnp.float32)
             turn[n] = part.reshape(rows * unit, lane)
 
@@ -293,8 +309,8 @@
         release(0, c)
         k = slot(0, c)
         for m in range(unit):
-            live = degree >= ids_ref[pl.ds(c * unit + m, 1), :]
-            for n, low in enumerate(range(0, channels, lane)):
+            live = degree >= ids_ref[pl.ds(lev_pos * slots + lax.div(c, split) * unit + m, 1), :]
+            for n, low in enumerate(range(0, width, lane)):
                 part = turn[n, pl.ds(m, rows, stride=unit), :]
                 part = jnp.where(live, part, 0.0)
                 mixed[k, m, pl.ds(0, rows), pl.ds(low, lane)] = part.astype(mixed.dtype)
@@ -340,10 +356,12 @@
             release(s + 1, c)
         for m in range(unit):
             total = jnp.dot(
-                factor[s * slots + c * unit + m][:, : 2 * rows], mixed[k, m], preferred_element_type=jnp.float32
+                factor[s * slots + lax.div(c, split) * unit + m][:, : 2 * rows],
+                mixed[k, m],
+                preferred_element_type=jnp.float32,
             )
             if last:
-                for n, low in enumerate(range(0, channels, lane)):
+                for n, low in enumerate(range(0, width, lane)):
                     turn[n, pl.ds(m, rows, stride=unit), :] = total[:, low : low + lane]
             else:
                 mixed[slot(s + 1, c), m, pl.ds(0, rows), :] = total.astype(mixed.dtype)
@@ -353,7 +371,7 @@
             pl.semaphore_signal(free_sem.at[s], inc=1, device_id={"wave": other(s)}, device_id_type=MESH)
 
         if last:
-            for n, low in enumerate(range(0, channels, lane)):
+            for n, low in enumerate(range(0, width, lane)):
                 ready[lax.rem(c, RING), :, :, pl.ds(low, lane)] = (
                     turn[n].astype(ready.dtype).reshape(rows, unit, lane)
                 )
@@ -368,6 +386,72 @@
         def _():
             mix(s, c)
 
+    piece = math.gcd(early, slots)
+    pieces = slots // piece
+    ahead, behind = early * lev_count, (slots - early) * lev_count
+    turnover = 2.0 * math.pi / longitudes
+
+    def tabulate(i):
+        owner, q = lax.div(i, pieces), lax.rem(i, pieces)
+        ids = ids_ref[pl.ds(pl.multiple_of(owner * slots + q * piece, piece), piece), :]
+        j = lax.broadcasted_iota(jnp.int32, ids.shape, 1)
+        a = lax.rem(lax.rem(ids * lane, longitudes) * j, longitudes).astype(jnp.float32) * turnover
+        b = lax.rem(ids * j, longitudes).astype(jnp.float32) * turnover
+        weight = jnp.where(ids == 0, 1.0, 2.0) * (2.0 * slots * lev_count) ** -0.5
+        cos_a, sin_a = weight * jnp.cos(a), weight * jnp.sin(a)
+        cos_b, sin_b = jnp.cos(b), jnp.sin(b)
+        first = q * piece < early
+        low = jnp.where(first, owner * early + q * piece, 2 * ahead + (q * piece - early) * lev_count + owner * piece)
+        high = low + jnp.where(first, ahead, behind)
+        low, high = pl.multiple_of(low, piece), pl.multiple_of(high, piece)
+        for n in range(longitudes // lane):
+            ca, sa = cos_a[:, n : n + 1], sin_a[:, n : n + 1]
+            columns = pl.ds(n * lane, lane)
+            table[pl.ds(low, piece), columns] = (ca * cos_b - sa * sin_b).astype(table.dtype)
+            table[pl.ds(high, piece), columns] = (-(sa * cos_b + ca * sin_b)).astype(table.dtype)
+
+    later_copy = pltpu.make_async_copy(table.at[pl.ds(2 * ahead, 2 * behind)], later_ref, table_sem)
+    tables = lev_count * pieces
+    table_at = sections
+    table_each = pl.cdiv(tables, early // unit * split - table_at)
+    early_chunks = early // unit * split
+    rows_at = early_chunks - 1 + RING + sections
+    rows_each = pl.cdiv(band, chunks + sections - rows_at)
+
+    def row_copy(r):
+        k = lax.rem(r, 2)
+        return pltpu.make_async_copy(bands_ref.at[r, :, pl.ds(0, early), :], row_in.at[k], row_sem.at[k])
+
+    def out_copy(r):
+        k = lax.rem(r, 2)
+        return pltpu.make_async_copy(row_out.at[k], partial_ref.at[r], out_sem.at[k])
+
+    def arrived(c, carry):
+        for d in range(1, lev_count):
+            band_copy(d, c, peer(lev_count - d)).wait_recv()
+        return carry
+
+    def synthesize(r):
+        k = lax.rem(r, 2)
+        row_copy(r).wait()
+
+        @pl.when(r + 1 < band)
+        def _():
+            row_copy(r + 1).start()
+
+        @pl.when(r >= 2)
+        def _():
+            out_copy(r - 2).wait()
+
+        turned = row_in[k].reshape(ahead, channels).T
+        spectrum = jnp.concatenate([turned[: channels // 2], turned[channels // 2 :]], axis=1)
+        span = math.gcd(longitudes, 512)
+        for j in range(0, longitudes, span):
+            row_out[k, :, pl.ds(j, span)] = jnp.dot(
+                spectrum, table[pl.ds(0, 2 * ahead), pl.ds(j, span)], preferred_element_type=jnp.float32
+            ).astype(row_out.dtype)
+        out_copy(r).start()
+
     pl.semaphore_wait(barrier, sections + lev_count - 1)
 
     def step(t, carry):
@@ -385,6 +469,27 @@
             prepare(t)
 
         guarded(sections - 1, t - sections)
+
+        for n in range(table_each):
+            i = (t - table_at) * table_each + n
+
+            @pl.when((i >= 0) & (i < tables))
+            def _():
+                tabulate(i)
+
+        @pl.when(t == rows_at)
+        def _():
+            later_copy.start()
+            lax.fori_loop(0, early_chunks, arrived, 0)
+            row_copy(0).start()
+
+        for n in range(rows_each):
+            r = (t - rows_at) * rows_each + n
+
+            @pl.when((r >= 0) & (r < band))
+            def _():
+                synthesize(r)
+
         return carry
 
     lax.fori_loop(0, chunks + sections, step, 0)
@@ -396,38 +501,47 @@
             band_copy(d, jnp.int32(c), lev_pos).wait_send()
         own_copy(jnp.int32(c)).wait()
 
-    def arrived(c, carry):
-        for d in range(1, lev_count):
-            band_copy(d, c, peer(lev_count - d)).wait_recv()
-        return carry
-
-    lax.fori_loop(0, chunks, arrived, 0)
+    lax.fori_loop(early_chunks, chunks, arrived, 0)
+    for r in range(band - 2, band):
+        out_copy(jnp.int32(r)).wait()
+    later_copy.wait()
 
 
 def exchange(ids, coefficients, factors, unit):
     lev_count = lax.axis_size("lev")
     rows, slots, channels = coefficients.shape
     sections = factors.shape[0]
-    chunks = slots // unit
+    chunks = slots // unit * SPLIT
+    width = channels // SPLIT
+    band = rows // lev_count
+    early = EARLY * unit
     kind = coefficients.dtype
     group = 16
+    behind = (slots - early) * lev_count
     return pl.pallas_call(
-        functools.partial(exchange_kernel, unit),
-        out_shape=jax.ShapeDtypeStruct((rows // lev_count, lev_count * slots, channels), kind),
+        functools.partial(exchange_kernel, unit, early),
+        out_shape=(
+            jax.ShapeDtypeStruct((band, lev_count, slots, channels), kind),
+            jax.ShapeDtypeStruct((band, channels // 2, NLON), kind),
+            jax.ShapeDtypeStruct((2 * behind, NLON), kind),
+        ),
         in_specs=[
             pl.BlockSpec(memory_space=pltpu.VMEM),
             pl.BlockSpec(memory_space=pltpu.HBM),
             pl.BlockSpec(memory_space=pltpu.HBM),
         ],
-        out_specs=pl.BlockSpec(memory_space=pltpu.HBM),
+        out_specs=[pl.BlockSpec(memory_space=pltpu.HBM)] * 3,
         scratch_shapes=[
-            pltpu.VMEM((2, rows, unit, channels), kind),
+            pltpu.VMEM((2, rows, unit, width), kind),
             pltpu.VMEM((2, 2, group, rows, slots), kind),
             pltpu.VMEM((2, slots * group, 128), jnp.float32),
             pltpu.VMEM((sections * slots, rows, 256), kind),
-            pltpu.VMEM((channels // 128, rows * unit, 128), jnp.float32),
-            pltpu.VMEM((sections * RING, unit, 2 * rows, channels), kind),
-            pltpu.VMEM((RING, rows, unit, channels), kind),
+            pltpu.VMEM((width // 128, rows * unit, 128), jnp.float32),
+            pltpu.VMEM((sections * RING, unit, 2 * rows, width), kind),
+            pltpu.VMEM((RING, rows, unit, width), kind),
+            pltpu.VMEM((2 * lev_count * slots, NLON), kind),
+            pltpu.VMEM((2, lev_count, early, channels), kind),
+            pltpu.VMEM((2, channels // 2, NLON), kind),
             pltpu.SemaphoreType.DMA((2,)),
             pltpu.SemaphoreType.DMA((2,)),
             pltpu.SemaphoreType.DMA((sections * RING,)),
@@ -435,6 +549,9 @@
             pltpu.SemaphoreType.DMA((RING, lev_count - 1)),
             pltpu.SemaphoreType.DMA((chunks, lev_count - 1)),
             pltpu.SemaphoreType.DMA((RING,)),
+            pltpu.SemaphoreType.DMA((2,)),
+            pltpu.SemaphoreType.DMA((2,)),
+            pltpu.SemaphoreType.DMA,
             pltpu.SemaphoreType.REGULAR((sections,)),
         ],
         compiler_params=pltpu.CompilerParams(
@@ -443,65 +560,50 @@
     )(ids, coefficients, factors)
 
 
-def grid_kernel(cos_a, sin_a, cos_b, sin_b, u_ref, out_ref, table):
-    slots = cos_a.shape[0]
+def finish_kernel(count, *refs):
+    partial_ref, table_ref, out_ref = refs[count:]
     half = out_ref.shape[1]
-    lane = cos_b.shape[1]
-
-    @pl.when(pl.program_id(0) == 0)
-    def _():
-        for j in range(out_ref.shape[2] // lane):
-            ca, sa = cos_a[:, j : j + 1], sin_a[:, j : j + 1]
-            table[:slots, j * lane : (j + 1) * lane] = (ca * cos_b[...] - sa * sin_b[...]).astype(table.dtype)
-            table[slots:, j * lane : (j + 1) * lane] = (-(sa * cos_b[...] + ca * sin_b[...])).astype(table.dtype)
-
-    turned = u_ref[0].T
+    channels = refs[0].shape[3]
+    wide = jnp.concatenate([ref[0].reshape(-1, channels) for ref in refs[:count]], axis=0)
+    turned = wide.T
     spectrum = jnp.concatenate([turned[:half], turned[half:]], axis=1)
     span = math.gcd(out_ref.shape[2], 512)
     for j in range(0, out_ref.shape[2], span):
-        out_ref[0, :, j : j + span] = jnp.dot(
-            spectrum, table[:, j : j + span], preferred_element_type=jnp.float32
-        ).astype(out_ref.dtype)
-
-
-def grid_of(wave_ids, bands):
-    rows, slots, channels = bands.shape
-    lane = 128
-
-    def angle(j):
-        phases = wave_ids[:, None] * j[None, :] % NLON
-        return phases.astype(jnp.float32) * (2.0 * math.pi / NLON)
-
-    weight = jnp.where(wave_ids == 0, 1.0, 2.0).astype(jnp.float32) / math.sqrt(2.0 * wave_ids.shape[0])
-    a = angle(lane * jnp.arange(NLON // lane, dtype=jnp.int32))
-    b = angle(jnp.arange(lane, dtype=jnp.int32))
-    parts = [weight[:, None] * jnp.cos(a), weight[:, None] * jnp.sin(a), jnp.cos(b), jnp.sin(b)]
+        total = jnp.dot(spectrum, table_ref[:, j : j + span], preferred_element_type=jnp.float32)
+        total += partial_ref[0, :, j : j + span].astype(jnp.float32)
+        out_ref[0, :, j : j + span] = total.astype(out_ref.dtype)
+
+
+def finish(bands, partial, table, early):
+    rows, owners, slots, channels = bands.shape
+    piece = math.gcd(early, slots)
+    starts = range(early // piece, slots // piece)
+    whole_row = pl.BlockSpec((1, *partial.shape[1:]), lambda i: (i, 0, 0))
     return pl.pallas_call(
-        grid_kernel,
+        functools.partial(finish_kernel, len(starts)),
         grid=(rows,),
-        out_shape=jax.ShapeDtypeStruct((rows, channels // 2, NLON), bands.dtype),
-        in_specs=[pl.BlockSpec(p.shape, lambda i: (0, 0), pipeline_mode=pl.Buffered(1)) for p in parts]
-        + [pl.BlockSpec((1, slots, channels), lambda i: (i, 0, 0))],
-        out_specs=pl.BlockSpec((1, channels // 2, NLON), lambda i: (i, 0, 0)),
-        scratch_shapes=[pltpu.VMEM((2 * slots, NLON), bands.dtype)],
+        out_shape=jax.ShapeDtypeStruct(partial.shape, partial.dtype),
+        in_specs=[pl.BlockSpec((1, owners, piece, channels), lambda i, n=n: (i, 0, n, 0)) for n in starts]
+        + [whole_row, pl.BlockSpec(table.shape, lambda i: (0, 0), pipeline_mode=pl.Buffered(1))],
+        out_specs=whole_row,
         cost_estimate=pl.CostEstimate(
-            flops=2 * rows * channels * slots * NLON,
-            bytes_accessed=2 * bands.size + rows * channels * NLON,
+            flops=2 * partial.size * table.shape[0],
+            bytes_accessed=2 * (2 * partial.size + table.size),
             transcendentals=0,
         ),
-    )(*parts, bands)
+    )(*[bands] * len(starts), partial, table)
 
 
 def unit_of(rows, slots):
-    return UNIT if rows % 16 == 0 and 128 <= 2 * rows <= 256 and slots % UNIT == 0 and slots // UNIT > RING else 0
+    return UNIT if rows % 16 == 0 and 128 <= 2 * rows <= 256 and slots % UNIT == 0 and slots // UNIT > EARLY + RING else 0
 
 
 def staged(coefficients, factors, wave_ids):
     rows, slots, _ = coefficients.shape
-    ids = lax.dynamic_slice_in_dim(wave_ids, lax.axis_index("lev") * slots, slots, 0)
-    ids = jnp.broadcast_to(ids[:, None], (slots, 128))
-    bands = exchange(ids, coefficients, factors, unit_of(rows, slots))
-    return grid_of(wave_ids, bands)
+    unit = unit_of(rows, slots)
+    ids = jnp.broadcast_to(wave_ids[:, None], (wave_ids.shape[0], 128))
+    bands, partial, table = exchange(ids, coefficients, factors, unit)
+    return finish(bands, partial, table, EARLY * unit)
 
 
 def solution(mesh):

time: 409 us -> 349 us (0.85)
  Pallas kernels: 399 us -> 344 us
  other arithmetic: 6.6 us -> 0 us
    pallas_call x2, Pallas kernels: 399 us -> 344 us  [the longest x1 312 us: exchange(): pl.pallas_call(functools.partial(exchange_kernel, unit, early), out_shape...]
where the time goes in v1:
time: 349 us; the launch traced here: 346 us
  Pallas kernels  344 us (99%)
    pallas_call x1, Pallas kernels, exchange(): pl.pallas_call(functools.partial(exchange_kernel, unit, early), out_shape...  312 us
    pallas_call x1, Pallas kernels, finish(): pl.pallas_call(functools.partial(finish_kernel, len(starts)), grid=(rows,...  32.3 us

profile of v1, /device:TPU:9, one launch (start us, length us, event | category | flops | bytes accessed | tf_op | source)
XLA Modules:
  0.0 345.8 jit_solution(9566935163035912574)
XLA Ops:
  0.0 1.6 broadcast_in_dim.2.ids_ref
  1.6 311.9 %shard_map.37 = (bf16[20,4,160,512]{3,2,1,0:T(8,128)(2,1)}, bf16[20,256,2560]{2,1,0:T(8,128)(2,1)}, bf16[512,2560]{1,0:T(8,128)(2,1)}) custom-call(s32[640,128]{1,0:T(8,128)} %broadcast_in_dim.2.ids_ref, bf16[80,160,512]{2,1,0:T(8,128)(2,1)} %coef_ref.1, bf16[3,2,80,80,160]{4,3,2,1,0:T(8,128)(2,1)} %factor_ref.1), custom_call_target="tpu_custom_call" | custom-call | tf_op jit(solution)/shard_map/pallas_call | solution.py:521
  313.5 32.3 %shard_map.38 = bf16[20,256,2560]{2,1,0:T(8,128)(2,1)} custom-call(bf16[20,4,160,512]{3,2,1,0:T(8,128)(2,1)} %get-tuple-element.8.refs_0_.refs_1_, bf16[20,4,160,512]{3,2,1,0:T(8,128)(2,1)} %get-tuple-element.8.refs_0_.refs_1_, bf16[20,256,2560]{2,1,0:T(8,128)(2,1)} %get-tuple-element.9.refs_2_, bf16[512,2560]{1,0:T(8,128)(2,1)} %get-tuple-element.10.refs_3_), custom_call_target="tpu_custom_call" | custom-call | flops 13421772800 | bytes 55050240 | tf_op jit(solution)/shard_map/pallas_call | solution.py:582

commit v2 on v1

--- a/solution.py
+++ b/solution.py
@@ -12,7 +12,8 @@
 NLON = 2560
 UNIT = 8
 SPLIT = 2
-EARLY = 12
+EARLY = 16
+TALL = 2
 
 
 def swapped(block, axis, apart):
@@ -216,6 +217,7 @@
     groups = rows // group
     jobs = sections * groups
     lane = 128
+    front = min(slots, lane)
 
     def other(s):
         bit = 1 << s
@@ -240,7 +242,7 @@
 
     def factor_copy(j):
         k = lax.rem(j, 2)
-        s, g = lax.div(j, groups), lax.rem(j, groups)
+        s, g = lax.div(lax.rem(j, jobs), groups), lax.rem(j, groups)
         return pltpu.make_async_copy(
             factor_ref.at[s, :, pl.ds(g * group, group)], factor_in.at[k], factor_sem.at[k]
         )
@@ -316,26 +318,34 @@
                 mixed[k, m, pl.ds(0, rows), pl.ds(low, lane)] = part.astype(mixed.dtype)
         send(0, c)
 
+    def rearrange(j, low, count):
+        s, g = lax.div(lax.rem(j, jobs), groups), lax.rem(j, groups)
+        k = lax.rem(j, 2)
+        factor_copy(j).wait()
+        for o in range(group):
+            both = jnp.concatenate(
+                [factor_in[k, q, o, :, pl.ds(low, count)] for q in range(2)]
+                + [jnp.zeros((2 * lane - 2 * rows, count), factor_in.dtype)],
+                axis=0,
+            )
+            for n in range(2):
+                factor_f32[n, pl.ds(o, count, stride=group), :] = (
+                    both[n * lane : (n + 1) * lane].T.astype(jnp.float32)
+                )
+
+        @pl.when(j + 2 < 2 * jobs)
+        def _():
+            factor_copy(j + 2).start()
+
+        row = pl.multiple_of(g * group, group)
+        for n in range(2):
+            factor[pl.ds(s * slots + low, count), pl.ds(row, group), pl.ds(n * lane, lane)] = (
+                factor_f32[n, pl.ds(0, count * group), :].astype(factor.dtype).reshape(count, group, lane)
+            )
+
     def prepare(s):
         def job(g, carry):
-            j = s * groups + g
-            factor_copy(j).wait()
-            k = lax.rem(j, 2)
-            for o in range(group):
-                both = jnp.concatenate([factor_in[k, 0, o], factor_in[k, 1, o]], axis=0)
-                rest = jnp.zeros((2 * lane - 2 * rows, slots), both.dtype)
-                for n, part in enumerate((both[:lane], jnp.concatenate([both[lane:], rest], axis=0))):
-                    factor_f32[n, pl.ds(o, slots, stride=group), :] = part.T.astype(jnp.float32)
-
-            @pl.when(j + 2 < jobs)
-            def _():
-                factor_copy(j + 2).start()
-
-            low = pl.multiple_of(g * group, group)
-            for n in range(2):
-                factor[pl.ds(s * slots, slots), pl.ds(low, group), pl.ds(n * lane, lane)] = (
-                    factor_f32[n].astype(factor.dtype).reshape(slots, group, lane)
-                )
+            rearrange(s * groups + g, 0, front)
             return carry
 
         lax.fori_loop(0, groups, job, 0)
@@ -469,6 +479,10 @@
             prepare(t)
 
         guarded(sections - 1, t - sections)
+
+        @pl.when((t > sections) & (t <= sections + jobs))
+        def _():
+            rearrange(jobs + t - sections - 1, front, slots - front)
 
         for n in range(table_each):
             i = (t - table_at) * table_each + n
@@ -534,7 +548,7 @@
         scratch_shapes=[
             pltpu.VMEM((2, rows, unit, width), kind),
             pltpu.VMEM((2, 2, group, rows, slots), kind),
-            pltpu.VMEM((2, slots * group, 128), jnp.float32),
+            pltpu.VMEM((2, 128 * group, 128), jnp.float32),
             pltpu.VMEM((sections * slots, rows, 256), kind),
             pltpu.VMEM((width // 128, rows * unit, 128), jnp.float32),
             pltpu.VMEM((sections * RING, unit, 2 * rows, width), kind),
@@ -562,28 +576,33 @@
 
 def finish_kernel(count, *refs):
     partial_ref, table_ref, out_ref = refs[count:]
-    half = out_ref.shape[1]
+    tall, half, longitudes = out_ref.shape
     channels = refs[0].shape[3]
-    wide = jnp.concatenate([ref[0].reshape(-1, channels) for ref in refs[:count]], axis=0)
-    turned = wide.T
-    spectrum = jnp.concatenate([turned[:half], turned[half:]], axis=1)
-    span = math.gcd(out_ref.shape[2], 512)
-    for j in range(0, out_ref.shape[2], span):
+    lines = []
+    for r in range(tall):
+        wide = jnp.concatenate([ref[r].reshape(-1, channels) for ref in refs[:count]], axis=0)
+        turned = wide.T
+        lines.append(jnp.concatenate([turned[:half], turned[half:]], axis=1))
+    spectrum = jnp.concatenate(lines, axis=0)
+    span = math.gcd(longitudes, 512)
+    for j in range(0, longitudes, span):
         total = jnp.dot(spectrum, table_ref[:, j : j + span], preferred_element_type=jnp.float32)
-        total += partial_ref[0, :, j : j + span].astype(jnp.float32)
-        out_ref[0, :, j : j + span] = total.astype(out_ref.dtype)
+        for r in range(tall):
+            own = total[r * half : (r + 1) * half] + partial_ref[r, :, j : j + span].astype(jnp.float32)
+            out_ref[r, :, j : j + span] = own.astype(out_ref.dtype)
 
 
 def finish(bands, partial, table, early):
     rows, owners, slots, channels = bands.shape
+    tall = math.gcd(rows, TALL)
     piece = math.gcd(early, slots)
     starts = range(early // piece, slots // piece)
-    whole_row = pl.BlockSpec((1, *partial.shape[1:]), lambda i: (i, 0, 0))
+    whole_row = pl.BlockSpec((tall, *partial.shape[1:]), lambda i: (i, 0, 0))
     return pl.pallas_call(
         functools.partial(finish_kernel, len(starts)),
-        grid=(rows,),
+        grid=(rows // tall,),
         out_shape=jax.ShapeDtypeStruct(partial.shape, partial.dtype),
-        in_specs=[pl.BlockSpec((1, owners, piece, channels), lambda i, n=n: (i, 0, n, 0)) for n in starts]
+        in_specs=[pl.BlockSpec((tall, owners, piece, channels), lambda i, n=n: (i, 0, n, 0)) for n in starts]
         + [whole_row, pl.BlockSpec(table.shape, lambda i: (0, 0), pipeline_mode=pl.Buffered(1))],
         out_specs=whole_row,
         cost_estimate=pl.CostEstimate(
@@ -595,7 +614,7 @@
 
 
 def unit_of(rows, slots):
-    return UNIT if rows % 16 == 0 and 128 <= 2 * rows <= 256 and slots % UNIT == 0 and slots // UNIT > EARLY + RING else 0
+    return UNIT if rows % 16 == 0 and 128 <= 2 * rows <= 256 and 128 < slots <= 256 and slots % UNIT == 0 and slots // UNIT > EARLY + RING else 0
 
 
 def staged(coefficients, factors, wave_ids):

time: 349 us -> 340 us (0.974)
  Pallas kernels: 344 us -> 334 us
    pallas_call x1, Pallas kernels: 32.3 us -> 23.9 us  [finish(): pl.pallas_call(functools.partial(finish_kernel, len(starts)), grid=(rows...]
where the time goes in v2:
time: 340 us; the launch traced here: 335 us
  Pallas kernels  334 us (98%)
    pallas_call x1, Pallas kernels, exchange(): pl.pallas_call(functools.partial(exchange_kernel, unit, early), out_shape...  310 us
    pallas_call x1, Pallas kernels, finish(): pl.pallas_call(functools.partial(finish_kernel, len(starts)), grid=(rows...  23.9 us

profile of v2, /device:TPU:9, one launch (start us, length us, event | category | flops | bytes accessed | tf_op | source)
XLA Modules:
  0.0 335.1 jit_solution(16632575527281340772)
XLA Ops:
  0.0 1.6 broadcast_in_dim.2.ids_ref
  1.6 309.7 %shard_map.37 = (bf16[20,4,160,512]{3,2,1,0:T(8,128)(2,1)}, bf16[20,256,2560]{2,1,0:T(8,128)(2,1)}, bf16[256,2560]{1,0:T(8,128)(2,1)}) custom-call(s32[640,128]{1,0:T(8,128)} %broadcast_in_dim.2.ids_ref, bf16[80,160,512]{2,1,0:T(8,128)(2,1)} %coef_ref.1, bf16[3,2,80,80,160]{4,3,2,1,0:T(8,128)(2,1)} %factor_ref.1), custom_call_target="tpu_custom_call" | custom-call | tf_op jit(solution)/shard_map/pallas_call | solution.py:535
  311.2 23.9 %shard_map.38 = bf16[20,256,2560]{2,1,0:T(8,128)(2,1)} custom-call(bf16[20,4,160,512]{3,2,1,0:T(8,128)(2,1)} %get-tuple-element.8.refs_0_, bf16[20,256,2560]{2,1,0:T(8,128)(2,1)} %get-tuple-element.9.refs_1_, bf16[256,2560]{1,0:T(8,128)(2,1)} %get-tuple-element.10.refs_2_), custom_call_target="tpu_custom_call" | custom-call | flops 6710886400 | bytes 53739520 | tf_op jit(solution)/shard_map/pallas_call | solution.py:601

commit v3 on v2

--- a/solution.py
+++ b/solution.py
@@ -13,7 +13,7 @@
 UNIT = 8
 SPLIT = 2
 EARLY = 16
-TALL = 2
+TALL = 4
 
 
 def swapped(block, axis, apart):
@@ -311,7 +311,7 @@
         release(0, c)
         k = slot(0, c)
         for m in range(unit):
-            live = degree >= ids_ref[pl.ds(lev_pos * slots + lax.div(c, split) * unit + m, 1), :]
+            live = degree >= ids_ref[lev_pos * slots + lax.div(c, split) * unit + m]
             for n, low in enumerate(range(0, width, lane)):
                 part = turn[n, pl.ds(m, rows, stride=unit), :]
                 part = jnp.where(live, part, 0.0)
@@ -403,7 +403,10 @@
 
     def tabulate(i):
         owner, q = lax.div(i, pieces), lax.rem(i, pieces)
-        ids = ids_ref[pl.ds(pl.multiple_of(owner * slots + q * piece, piece), piece), :]
+        line = lax.broadcasted_iota(jnp.int32, (piece, lane), 0)
+        ids = jnp.zeros((piece, lane), jnp.int32)
+        for n in range(piece):
+            ids = jnp.where(line == n, ids_ref[owner * slots + q * piece + n], ids)
         j = lax.broadcasted_iota(jnp.int32, ids.shape, 1)
         a = lax.rem(lax.rem(ids * lane, longitudes) * j, longitudes).astype(jnp.float32) * turnover
         b = lax.rem(ids * j, longitudes).astype(jnp.float32) * turnover
@@ -464,12 +467,21 @@
 
     pl.semaphore_wait(barrier, sections + lev_count - 1)
 
+    def reach(t, jump):
+        ahead_of = jnp.where(t > jump, t + 1, t)
+        return jnp.minimum(jnp.maximum(ahead_of, 0), chunks)
+
     def step(t, carry):
-        guarded(0, t - 1)
-
-        @pl.when(t < chunks)
-        def _():
-            begin(t)
+        def first(c, carry):
+            mix(0, c)
+            return carry
+
+        def fresh(c, carry):
+            begin(c)
+            return carry
+
+        lax.fori_loop(reach(t - 1, 5), reach(t, 5), first, 0)
+        lax.fori_loop(reach(t, 5), reach(t + 1, 5), fresh, 0)
 
         for s in range(1, sections - 1):
             guarded(s, t - 1 - s)
@@ -540,7 +552,7 @@
             jax.ShapeDtypeStruct((2 * behind, NLON), kind),
         ),
         in_specs=[
-            pl.BlockSpec(memory_space=pltpu.VMEM),
+            pl.BlockSpec(memory_space=pltpu.SMEM),
             pl.BlockSpec(memory_space=pltpu.HBM),
             pl.BlockSpec(memory_space=pltpu.HBM),
         ],
@@ -620,8 +632,7 @@
 def staged(coefficients, factors, wave_ids):
     rows, slots, _ = coefficients.shape
     unit = unit_of(rows, slots)
-    ids = jnp.broadcast_to(wave_ids[:, None], (wave_ids.shape[0], 128))
-    bands, partial, table = exchange(ids, coefficients, factors, unit)
+    bands, partial, table = exchange(wave_ids, coefficients, factors, unit)
     return finish(bands, partial, table, EARLY * unit)
 
 

time: 340 us -> 337 us (level)
  no operation moved by 1% of the time
where the time goes in v3:
time: 337 us; the launch traced here: 332 us
  Pallas kernels  332 us (99%)
    pallas_call x1, Pallas kernels, exchange(): pl.pallas_call(functools.partial(exchange_kernel, unit, early), out_shape...  310 us
    pallas_call x1, Pallas kernels, finish(): pl.pallas_call(functools.partial(finish_kernel, len(starts)), grid=(rows...  22.7 us

profile of v3, /device:TPU:9, one launch (start us, length us, event | category | flops | bytes accessed | tf_op | source)
XLA Modules:
  0.0 332.2 jit_solution(17979222080905777975)
XLA Ops:
  0.0 309.5 %shard_map.37 = (bf16[20,4,160,512]{3,2,1,0:T(8,128)(2,1)}, bf16[20,256,2560]{2,1,0:T(8,128)(2,1)}, bf16[256,2560]{1,0:T(8,128)(2,1)}) custom-call(s32[640]{0:T(1024)} %ids_ref.1, bf16[80,160,512]{2,1,0:T(8,128)(2,1)} %coef_ref.1, bf16[3,2,80,80,160]{4,3,2,1,0:T(8,128)(2,1)} %factor_ref.1), custom_call_target="tpu_custom_call" | custom-call | tf_op jit(solution)/shard_map/pallas_call | solution.py:547
  309.5 22.7 %shard_map.38 = bf16[20,256,2560]{2,1,0:T(8,128)(2,1)} custom-call(bf16[20,4,160,512]{3,2,1,0:T(8,128)(2,1)} %get-tuple-element.8.refs_0_, bf16[20,256,2560]{2,1,0:T(8,128)(2,1)} %get-tuple-element.9.refs_1_, bf16[256,2560]{1,0:T(8,128)(2,1)} %get-tuple-element.10.refs_2_), custom_call_target="tpu_custom_call" | custom-call | flops 6710886400 | bytes 53739520 | tf_op jit(solution)/shard_map/pallas_call | solution.py:613
